TPU v7x, 256 devices: a whole 4x4x8 slice. The times are simulated.
256 devices in a mesh: order: 64 (over z, x, core), lat: 4 (over y).
Axes of the slice: x: 4, y: 4, z: 8, core: 2. Of those that a mesh axis runs over, the one named last changes fastest.
Arguments:
- position: float32 [128, 2, 64, 2160], P('order', None, None, 'lat'), may hold values from -6 to 6
- residual: float32 [128, 2, 64, 2160], P('order', None, None, 'lat'), as said below
- direction: float32 [128, 2, 64, 2160], P('order', None, None, 'lat'), as said below
- legendre: float32 [128, 2160, 2048], P('order', None, 'lat'), may hold values from -0.125 to 0.125
- order_of: int32 [128], replicated, may hold values from 0 to 2032, as said below
- class_idx: int32 [2048, 4320], P(('lat', 'order')), may hold values from 0 to 15
- land: int32 [2048, 4320], P(('lat', 'order')), may hold values 0 or 1
- class_weight: float32 [16, 2], replicated, may hold values from 0.2 to 5
- damping: float32 [2160], P('lat'), may hold values from 0.05 to 0.5
Outputs:
- new_position: float32 [128, 2, 64, 2160], P('order', None, None, 'lat')
- new_residual: float32 [128, 2, 64, 2160], P('order', None, None, 'lat')
- new_direction: float32 [128, 2, 64, 2160], P('order', None, None, 'lat')
Inputs may be any that keep to these rules, and one draw needn't show every extreme that they name: `order_of`: distinct multiples of 16: each of 0, 16, ..., 16 * (128 - 1) appears exactly once. `residual`: real-valued and not zero. `direction`: real-valued and not zero.
All inputs are finite; a program needn't handle non-finite values. No bound on the sum of `land` on one device may be relied on, other than what follows from the above.
Results may differ from a plain program's by a relative error of at most 0.000058.
Values sent between devices are 32-bit elements; how exact they have to be, the bound alone decides.
A program may use at most 128 MiB of HBM per device.

v0:
```python
import math
import jax
import jax.numpy as jnp
from jax import lax
from jax.sharding import PartitionSpec as P


def tables(order_of, longitudes):
    longitude = jnp.arange(longitudes, dtype=jnp.int32)
    phases = order_of[:, None] * longitude[None, :] % longitudes
    angles = phases.astype(jnp.float32) * (2.0 * math.pi / longitudes)
    return jnp.stack([jnp.cos(angles), jnp.sin(angles)])


def sample_sums(product):
    return jnp.sum(product, axis=(0, 1, 3))


def shards(
    position, residual, direction, legendre, order_of, class_idx, land, class_weight, damping
):
    highest = lax.Precision.HIGHEST
    m_local = position.shape[0]
    samples = position.shape[2]
    deg_local = position.shape[3]
    band_rows = legendre.shape[2]
    lat_index = lax.axis_index("lat")
    order_index = lax.axis_index("order")
    my_orders = lax.dynamic_slice_in_dim(order_of, order_index * m_local, m_local)
    deg_start = lat_index * deg_local
    own_degrees = deg_start + jnp.arange(deg_local, dtype=jnp.int32)
    own_valid = (own_degrees[None, :] >= my_orders[:, None]).astype(jnp.float32)[:, None, None, :]
    pos_m = position * own_valid
    res_m = residual * own_valid
    dir_m = direction * own_valid
    norm_before = lax.psum(sample_sums(res_m * res_m), ("order", "lat"))
    block_part = lax.all_gather(direction, "lat", axis=3, tiled=True)
    degree_count = block_part.shape[3]
    in_block = jnp.arange(degree_count, dtype=jnp.int32)
    in_triangle = (in_block[None, :] >= my_orders[:, None]).astype(jnp.float32)
    masked = block_part * in_triangle[:, None, None, :]
    synthesis = jnp.einsum("mskd,mdt->mtsk", masked, legendre, precision=highest)
    grid_in = lax.all_to_all(
        synthesis.reshape(m_local, band_rows, 2 * samples),
        "order",
        split_axis=1,
        concat_axis=0,
        tiled=True,
    )
    orders_all = grid_in.shape[0]
    rows_here = grid_in.shape[1]
    grid_in = grid_in.reshape(orders_all, rows_here, 2, samples)
    longitudes = class_idx.shape[1]
    harmonic = tables(order_of, longitudes)
    surface = jnp.einsum("mrsk,sml->rkl", grid_in, harmonic, precision=highest)
    class_count = class_weight.shape[0]
    onehot = (
        class_idx[:, :, None] == jnp.arange(class_count, dtype=jnp.int32)[None, None, :]
    ).astype(jnp.float32)
    by_class = jnp.dot(onehot, class_weight, precision=highest)
    weight_grid = jnp.where(land == 1, by_class[:, :, 1], by_class[:, :, 0])
    weighted = surface * weight_grid[:, None, :]
    spectra = jnp.einsum("rkl,sml->mrsk", weighted, harmonic, precision=highest) * (
        2.0 / longitudes
    )
    returned = lax.all_to_all(
        spectra.reshape(orders_all, rows_here, 2 * samples),
        "order",
        split_axis=0,
        concat_axis=1,
        tiled=True,
    )
    returned = returned.reshape(m_local, band_rows, 2, samples)
    band_part = jnp.einsum("mtsk,mdt->mskd", returned, legendre, precision=highest)
    totals = lax.psum(band_part, "lat")
    summed = lax.dynamic_slice_in_dim(totals, deg_start, deg_local, 3)
    applied = (summed + damping[None, None, None, :] * dir_m) * own_valid
    curvature_sum = lax.psum(sample_sums(dir_m * applied), ("order", "lat"))
    step_size = (norm_before / curvature_sum)[None, None, :, None]
    new_residual = res_m - step_size * applied
    norm_after = lax.psum(sample_sums(new_residual * new_residual), ("order", "lat"))
    ratio_new = (norm_after / norm_before)[None, None, :, None]
    new_position = pos_m + step_size * dir_m
    new_direction = new_residual + ratio_new * dir_m
    return (new_position, new_residual, new_direction)


def solution(mesh):
    return jax.shard_map(
        shards,
        mesh=mesh,
        in_specs=(
            P("order", None, None, "lat"),
            P("order", None, None, "lat"),
            P("order", None, None, "lat"),
            P("order", None, "lat"),
            P(),
            P(("lat", "order"), None),
            P(("lat", "order"), None),
            P(),
            P("lat"),
        ),
        out_specs=(
            P("order", None, None, "lat"),
            P("order", None, None, "lat"),
            P("order", None, None, "lat"),
        ),
        check_vma=False,
    )
```

profile of v0, /device:TPU:1, one launch (start us, length us, event | category | flops | bytes accessed | tf_op | source)
XLA Modules:
  0.0 419.9 jit_solution(14200132624685688203)
XLA Ops:
  7.2 2.3 copy.20
  9.7 0.7 fusion.11
  10.6 0.9 fusion.37
  11.4 9.9 %fusion.17 = (f32[1,128,4320]{1,2,0:T(8,128)S(1)}, f32[1,128,4320]{1,2,0:T(8,128)}) fusion(s32[128]{0:T(128)S(1)} %copy-done.10), kind=kLoop, calls=%fused_computation.23 | loop fusion | flops 4976640 | bytes 4424192 | tf_op jit(solution)/shard_map/cos | solution.py:12
  21.3 44.9 %all-gather.2.cloned.1.call-done = f32[2,2,64,2160]{2,1,0,3:T(2,128)} async-done(((f32[2,2,64,540]{2,1,0,3:T(2,128)}), f32[2,2,64,2160]{2,1,0,3:T(2,128)}) %all-gather.2.cloned.1.call-update) | async-done | bytes 2211856 | tf_op jit(solution)/shard_map/all_gather | solution.py:37
  66.2 6.6 %broadcast_multiply_fusion = f32[2,2,64,2160]{2,1,0,3:T(2,128)S(1)} fusion(f32[2,2,64,2160]{2,1,0,3:T(2,128)} %all-gather.2.cloned.1.call-done, f32[2,2160]{0,1:T(8,128)S(1)} %fusion.30), kind=kLoop, calls=%fused_computation.18 | loop fusion | flops 552960 | bytes 4440960 | tf_op jit(solution)/shard_map/mul | solution.py:41
  72.8 8.7 %fusion.4 = f32[2,2,64,512]{3,2,1,0:T(8,128)S(1)} fusion(f32[2,2160,512]{2,1,0:T(8,128)S(1)} %copy-done.1, f32[2,2,64,2160]{2,1,0,3:T(2,128)S(1)} %broadcast_multiply_fusion), kind=kOutput, calls=%fused_computation.5 | convolution fusion | flops 3397386240 | bytes 11583488 | tf_op jit(solution)/shard_map/mskd,mdt->mtsk/dot_general | solution.py:42
  81.5 1.0 copy.22
  82.5 10.8 %all-to-all-start = ((f32[2,512,128]{2,0,1:T(2,128)}), f32[2,512,128]{2,0,1:T(2,128)S(1)}, u32[]{:S(2)}, u32[]{:S(2)}) async-start(f32[2,512,128]{2,0,1:T(2,128)} %copy.22), calls=%async_computation | async-start | bytes 1048576 | tf_op jit(solution)/shard_map/all_to_all | solution.py:43
  93.6 17.4 %all-to-all-done = f32[2,512,128]{2,0,1:T(2,128)S(1)} async-done(((f32[2,512,128]{2,0,1:T(2,128)}), f32[2,512,128]{2,0,1:T(2,128)S(1)}, u32[]{:S(2)}, u32[]{:S(2)}) %all-to-all-start) | async-done | bytes 524320 | tf_op jit(solution)/shard_map/all_to_all | solution.py:43
  111.0 0.8 copy.24
  111.9 1.6 reshape.148
  113.5 31.3 %fusion.8 = f32[8,64,4320,1]{2,1,3,0:T(8,128)S(1)} fusion(f32[1,128,4320]{1,2,0:T(8,128)} %get-tuple-element.13, f32[1,128,4320]{1,2,0:T(8,128)S(1)} %get-tuple-element.12, f32[128,8,2,64]{3,2,1,0:T(2,128)S(1)} %reshape.148), kind=kOutput, calls=%fused_computation.10 | convolution fusion | flops 6795878400 | bytes 13795328 | tf_op jit(solution)/shard_map/mrsk,sml->rkl/dot_general | solution.py:55
  144.8 7.8 %fusion.24 = f32[128,8,2,64]{0,3,1,2:T(8,128)S(1)} fusion(f32[8,64,4320,1]{2,1,3,0:T(8,128)S(1)} %fusion.8, f32[8,4320]{1,0:T(8,128)S(1)} %fusion.33, f32[1,128,4320]{1,2,0:T(8,128)S(1)} %copy-done.2, f32[1,128,4320]{1,2,0:T(8,128)S(1)} %get-tuple-element.12), kind=kOutput, calls=%fused_computation.26 | convolution fusion | flops 6798221312 | bytes 13933568 | tf_op jit(solution)/shard_map/rkl,sml->mrsk/dot_general | solution.py:63
  152.7 0.2 copy.28
  153.0 23.3 %all_to_all.30 = f32[128,8,128]{2,1,0:T(8,128)S(1)} all-to-all(f32[128,8,128]{2,1,0:T(8,128)S(1)} %copy.28), channel_id=1, replica_groups=mesh['order'=64,'lat'=4] {'order'}, dimensions={0} | all-to-all | bytes 1048576 | tf_op jit(solution)/shard_map/all_to_all | solution.py:66
  176.3 0.6 reshape.150
  176.9 19.2 %fusion.2 = f32[2,2,64,2160]{3,2,1,0:T(8,128)} fusion(f32[2,2160,512]{2,1,0:T(8,128)} %param.12, f32[2,512,2,64]{3,2,1,0:T(2,128)S(1)} %reshape.150), kind=kOutput, calls=%fused_computation.3 | convolution fusion | flops 3397386240 | bytes 11583488 | tf_op jit(solution)/shard_map/mtsk,mdt->mskd/dot_general | solution.py:74
  196.3 61.3 %all-reduce.3.cloned.1.call-done = f32[2,2,64,2160]{3,2,1,0:T(8,128)} async-done(((f32[2,2,64,2160]{3,2,1,0:T(8,128)}), f32[2,2,64,2160]{3,2,1,0:T(8,128)}) %all-reduce.3.cloned.1.call-update) | async-done | bytes 2211856 | tf_op jit(solution)/shard_map/psum | solution.py:75
  257.6 1.6 multiply_reduce_fusion.1
  259.2 76.0 %all-reduce = (f32[64]{0:T(128)S(1)}, f32[64]{0:T(128)S(1)}) all-reduce(f32[64]{0:T(128)S(1)} %get-tuple-element.4, f32[64]{0:T(128)S(1)} %get-tuple-element.3), channel_id=1, replica_groups=mesh['order'=64,'lat'=4] {'order','lat'}, use_global_device_ids=true, to_apply=%region_1.0 | all-reduce | flops 128 | bytes 1024 | tf_op jit(solution)/shard_map/psum | solution.py:36
  335.1 2.5 multiply_reduce_fusion
  337.6 74.3 %psum.31 = f32[64]{0:T(128)S(1)} all-reduce(f32[64]{0:T(128)S(1)} %get-tuple-element.7), channel_id=1, replica_groups=mesh['order'=64,'lat'=4] {'order','lat'}, use_global_device_ids=true, to_apply=%region_6.7 | all-reduce | flops 64 | bytes 512 | tf_op jit(solution)/shard_map/psum | solution.py:81
  411.9 1.0 multiply_add_fusion
  (38 shorter events, 0.8 us)
Async XLA Ops:
  7.2 2.5 copy-start
  7.2 2.4 copy-start.10
  7.2 2.5 copy-start.11
  7.2 59.0 %all-gather.2.cloned.1.call-start = ((), (), s32[]{:S(2)}) async-start(), calls=%async_computation.2 | async-start | bytes 5529600 | tf_op jit(solution)/shard_map/all_gather | solution.py:37
  66.2 6.6 %copy-start.1 = (f32[2,2160,512]{2,1,0:T(8,128)S(1)}, f32[2,2160,512]{2,1,0:T(8,128)}, u32[]{:S(2)}) copy-start(f32[2,2160,512]{2,1,0:T(8,128)} %param.12) | copy-start | bytes 26542084
  72.7 20.8 %copy-start.7 = (f32[8,4320,1]{1,2,0:T(1,128)S(1)}, f32[8,4320,1]{1,2,0:T(1,128)}, u32[]{:S(2)}) copy-start(f32[8,4320,1]{1,2,0:T(1,128)} %get-tuple-element.11) | copy-start | bytes 414724
  72.8 20.8 %copy-start.8 = (s32[8,4320]{1,0:T(8,128)S(1)}, s32[8,4320]{1,0:T(8,128)}, u32[]{:S(2)}) copy-start(s32[8,4320]{1,0:T(8,128)} %param.15) | copy-start | bytes 414724
  82.5 28.5 %all-to-all-start = ((f32[2,512,128]{2,0,1:T(2,128)}), f32[2,512,128]{2,0,1:T(2,128)S(1)}, u32[]{:S(2)}, u32[]{:S(2)}) async-start(f32[2,512,128]{2,0,1:T(2,128)} %copy.22), calls=%async_computation | async-start | bytes 1048576 | tf_op jit(solution)/shard_map/all_to_all | solution.py:43
  93.3 164.3 %all-reduce.3.cloned.1.call-start = ((), (), s32[]{:S(2)}) async-start(), calls=%async_computation.3 | async-start | bytes 4456448 | tf_op jit(solution)/shard_map/psum | solution.py:75
  113.5 31.3 %copy-start.2 = (f32[1,128,4320]{1,2,0:T(8,128)S(1)}, f32[1,128,4320]{1,2,0:T(8,128)}, u32[]{:S(2)}) copy-start(f32[1,128,4320]{1,2,0:T(8,128)} %get-tuple-element.13) | copy-start | bytes 6635524
  196.2 61.4 %copy-start.3 = (f32[2,2,64,540]{3,2,1,0:T(8,128)S(1)}, f32[2,2,64,540]{3,2,1,0:T(8,128)}, u32[]{:S(2)}) copy-start(f32[2,2,64,540]{3,2,1,0:T(8,128)} %param.11) | copy-start | bytes 1658884
  196.2 61.4 %copy-start.4 = (f32[2,2,64,540]{3,2,1,0:T(8,128)S(1)}, f32[2,2,64,540]{3,2,1,0:T(8,128)}, u32[]{:S(2)}) copy-start(f32[2,2,64,540]{3,2,1,0:T(8,128)} %param.10) | copy-start | bytes 1658884
  196.2 61.4 %copy-start.9 = (f32[540]{0:T(1024)S(1)}, f32[540]{0:T(1024)}, u32[]{:S(2)}) copy-start(f32[540]{0:T(1024)} %param.17) | copy-start | bytes 6484
  196.2 138.9 %copy-start.6 = (f32[2,2,64,540]{3,2,1,0:T(8,128)S(1)}, f32[2,2,64,540]{3,2,1,0:T(8,128)}, u32[]{:S(2)}) copy-start(f32[2,2,64,540]{3,2,1,0:T(8,128)} %param.9) | copy-start | bytes 1658884
  337.6 75.3 %copy-start.5 = (f32[2,2,64,540]{3,2,1,0:T(8,128)}, f32[2,2,64,540]{3,2,1,0:T(8,128)S(1)}, u32[]{:S(2)}) copy-start(f32[2,2,64,540]{3,2,1,0:T(8,128)S(1)} %get-tuple-element.8) | copy-start | bytes 1658884
Sparse Core Ops, SparseCore 0:
  9.8 56.2 all-gather.1
  196.3 61.1 all-reduce.2
where the time goes:
time: 429 us; the launch traced here: 420 us
  blocking collectives  174 us (41%)
  waiting for transfers between devices  124 us (29%)
  matrix products  67.8 us (16%)
  other arithmetic  21.7 us (5%)
  between operations  14.5 us (3%)
  starting transfers between devices  11.1 us (3%)
  local copies, waits for them, and re-layouts  7.76 us (2%)
    psum x1, blocking collectives, shards(): norm_before = lax.psum(sample_sums(res_m * res_m), ('order', 'lat'))  76 us
    psum x1, blocking collectives, shards(): lax.psum(sample_sums(new_residual * new_residual), ('order', 'lat'))  74.3 us
    psum x1, waiting for transfers between devices, shards(): totals = lax.psum(band_part, 'lat')  61.3 us
    all_gather x1, waiting for transfers between devices, shards(): block_part = lax.all_gather(direction, 'lat', axis=3, tiled=True)  44.9 us
    dot_general x1, matrix products, shards(): surface = jnp.einsum('mrsk,sml->rkl', grid_in, harmonic, precision=highest)  31.3 us
    all_to_all x1, blocking collectives, shards(): lax.all_to_all(spectra.reshape(orders_all, rows_here, 2 * samples), 'orde...  23.3 us
    dot_general x1, matrix products, shards(): jnp.einsum('mtsk,mdt->mskd', returned, legendre, precision=highest)  19.2 us
    all_to_all x1, waiting for transfers between devices, shards(): lax.all_to_all(synthesis.reshape(m_local, band_rows, 2 * samples), 'order...  17.4 us
  transfers between devices with their start and end apart: 3, of which 3 were waited for; matrix products, arithmetic and copies ran while one was open for 3% of the time, Pallas kernels for 0%

commit v1 on v0

--- a/solution.py
+++ b/solution.py
@@ -72,7 +72,9 @@
     )
     returned = returned.reshape(m_local, band_rows, 2, samples)
     band_part = jnp.einsum("mtsk,mdt->mskd", returned, legendre, precision=highest)
-    totals = lax.psum(band_part, "lat")
+    totals = band_part
+    for hop in (1, 2):
+        totals = totals + lax.ppermute(totals, "lat", [(dev, dev ^ hop) for dev in range(4)])
     summed = lax.dynamic_slice_in_dim(totals, deg_start, deg_local, 3)
     applied = (summed + damping[None, None, None, :] * dir_m) * own_valid
     curvature_sum = lax.psum(sample_sums(dir_m * applied), ("order", "lat"))

time: 429 us -> 467 us (1.089)
  waiting for transfers between devices: 124 us -> 159 us
    ppermute x0 -> x2, waiting for transfers between devices: none -> 96.8 us  [shards(): lax.ppermute(totals, 'lat', [(dev, dev ^ hop) for dev in range(4)])]
    psum x1 -> x0, waiting for transfers between devices: 61.3 us -> none  [shards(): totals = lax.psum(band_part, 'lat')]
  transfers between devices with their start and end apart: 3 -> 4, of which waited for: 3 -> 4; matrix products, arithmetic and copies ran while one was open for 3% -> 3% of each run, Pallas kernels for 0% -> 0%
where the time goes in v1:
time: 467 us; the launch traced here: 458 us
  blocking collectives  171 us (37%)
  waiting for transfers between devices  159 us (34%)
  matrix products  66.6 us (14%)
  other arithmetic  24.8 us (5%)
  between operations  14.5 us (3%)
  starting transfers between devices  13.6 us (3%)
  local copies, waits for them, and re-layouts  8.27 us (2%)
    ppermute x2, waiting for transfers between devices, shards(): lax.ppermute(totals, 'lat', [(dev, dev ^ hop) for dev in range(4)])  96.8 us
    psum x1, blocking collectives, shards(): norm_before = lax.psum(sample_sums(res_m * res_m), ('order', 'lat'))  74.4 us
    psum x1, blocking collectives, shards(): lax.psum(sample_sums(new_residual * new_residual), ('order', 'lat'))  73.3 us
    all_gather x1, waiting for transfers between devices, shards(): block_part = lax.all_gather(direction, 'lat', axis=3, tiled=True)  44.9 us
    dot_general x1, matrix products, shards(): surface = jnp.einsum('mrsk,sml->rkl', grid_in, harmonic, precision=highest)  31.3 us
    all_to_all x1, blocking collectives, shards(): lax.all_to_all(spectra.reshape(orders_all, rows_here, 2 * samples), 'orde...  23.3 us
    dot_general x1, matrix products, shards(): jnp.einsum('mtsk,mdt->mskd', returned, legendre, precision=highest)  18.1 us
    all_to_all x1, waiting for transfers between devices, shards(): lax.all_to_all(synthesis.reshape(m_local, band_rows, 2 * samples), 'order...  17.5 us
  transfers between devices with their start and end apart: 4, of which 4 were waited for; matrix products, arithmetic and copies ran while one was open for 3% of the time, Pallas kernels for 0%

profile of v1, /device:TPU:1, one launch (start us, length us, event | category | flops | bytes accessed | tf_op | source)
XLA Modules:
  0.0 457.9 jit_solution(4965045944011876179)
XLA Ops:
  7.2 2.3 copy.20
  9.7 0.7 fusion.11
  10.6 0.9 fusion.39
  11.4 9.8 %fusion.17 = (f32[1,128,4320]{1,2,0:T(8,128)S(1)}, f32[1,128,4320]{1,2,0:T(8,128)}) fusion(s32[128]{0:T(128)S(1)} %copy-done.10), kind=kLoop, calls=%fused_computation.23 | loop fusion | flops 4976640 | bytes 4424192 | tf_op jit(solution)/shard_map/cos | solution.py:12
  21.3 44.9 %all-gather.2.cloned.1.call-done = f32[2,2,64,2160]{2,1,0,3:T(2,128)} async-done(((f32[2,2,64,540]{2,1,0,3:T(2,128)}), f32[2,2,64,2160]{2,1,0,3:T(2,128)}) %all-gather.2.cloned.1.call-update) | async-done | bytes 2211856 | tf_op jit(solution)/shard_map/all_gather | solution.py:37
  66.2 6.6 %broadcast_multiply_fusion = f32[2,2,64,2160]{2,1,0,3:T(2,128)S(1)} fusion(f32[2,2,64,2160]{2,1,0,3:T(2,128)} %all-gather.2.cloned.1.call-done, f32[2,2160]{0,1:T(8,128)S(1)} %fusion.30), kind=kLoop, calls=%fused_computation.18 | loop fusion | flops 552960 | bytes 4440960 | tf_op jit(solution)/shard_map/mul | solution.py:41
  72.8 8.7 %fusion.4 = f32[2,2,64,512]{3,2,1,0:T(8,128)S(1)} fusion(f32[2,2160,512]{2,1,0:T(8,128)S(1)} %copy-done.1, f32[2,2,64,2160]{2,1,0,3:T(2,128)S(1)} %broadcast_multiply_fusion), kind=kOutput, calls=%fused_computation.5 | convolution fusion | flops 3397386240 | bytes 11583488 | tf_op jit(solution)/shard_map/mskd,mdt->mtsk/dot_general | solution.py:42
  81.5 1.0 copy.22
  82.5 11.0 %all-to-all-start = ((f32[2,512,128]{2,0,1:T(2,128)}), f32[2,512,128]{2,0,1:T(2,128)S(1)}, u32[]{:S(2)}, u32[]{:S(2)}) async-start(f32[2,512,128]{2,0,1:T(2,128)} %copy.22), calls=%async_computation | async-start | bytes 1048576 | tf_op jit(solution)/shard_map/all_to_all | solution.py:43
  93.5 17.5 %all-to-all-done = f32[2,512,128]{2,0,1:T(2,128)S(1)} async-done(((f32[2,512,128]{2,0,1:T(2,128)}), f32[2,512,128]{2,0,1:T(2,128)S(1)}, u32[]{:S(2)}, u32[]{:S(2)}) %all-to-all-start) | async-done | bytes 524320 | tf_op jit(solution)/shard_map/all_to_all | solution.py:43
  111.0 0.8 copy.24
  111.9 1.6 reshape.148
  113.5 31.3 %fusion.8 = f32[8,64,4320,1]{2,1,3,0:T(8,128)S(1)} fusion(f32[1,128,4320]{1,2,0:T(8,128)} %get-tuple-element.13, f32[1,128,4320]{1,2,0:T(8,128)S(1)} %get-tuple-element.12, f32[128,8,2,64]{3,2,1,0:T(2,128)S(1)} %reshape.148), kind=kOutput, calls=%fused_computation.10 | convolution fusion | flops 6795878400 | bytes 13795328 | tf_op jit(solution)/shard_map/mrsk,sml->rkl/dot_general | solution.py:55
  144.8 7.8 %fusion.24 = f32[128,8,2,64]{0,3,1,2:T(8,128)S(1)} fusion(f32[8,64,4320,1]{2,1,3,0:T(8,128)S(1)} %fusion.8, f32[8,4320]{1,0:T(8,128)S(1)} %fusion.35, f32[1,128,4320]{1,2,0:T(8,128)S(1)} %copy-done.2, f32[1,128,4320]{1,2,0:T(8,128)S(1)} %get-tuple-element.12), kind=kOutput, calls=%fused_computation.26 | convolution fusion | flops 6798221312 | bytes 13933568 | tf_op jit(solution)/shard_map/rkl,sml->mrsk/dot_general | solution.py:63
  153.0 23.3 %all_to_all.30 = f32[128,8,128]{2,1,0:T(8,128)S(1)} all-to-all(f32[128,8,128]{2,1,0:T(8,128)S(1)} %copy.28), channel_id=1, replica_groups=mesh['order'=64,'lat'=4] {'order'}, dimensions={0} | all-to-all | bytes 1048576 | tf_op jit(solution)/shard_map/all_to_all | solution.py:66
  176.9 18.1 %fusion.2 = f32[2,2,64,2160]{3,2,1,0:T(8,128)S(1)} fusion(f32[2,2160,512]{2,1,0:T(8,128)} %param.12, f32[2,512,2,64]{3,2,1,0:T(2,128)S(1)} %reshape.150), kind=kOutput, calls=%fused_computation.3 | convolution fusion | flops 3397386240 | bytes 11583488 | tf_op jit(solution)/shard_map/mtsk,mdt->mskd/dot_general | solution.py:74
  195.7 49.0 %collective-permute-done = f32[2,2,64,2160]{3,2,1,0:T(8,128)S(1)} collective-permute-done((f32[2,2,64,2160]{3,2,1,0:T(8,128)S(1)}, f32[2,2,64,2160]{3,2,1,0:T(8,128)S(1)}, u32[]{:S(2)}, u32[]{:S(2)}) %collective-permute-start) | collective-permute-done | bytes 2211872 | tf_op jit(solution)/shard_map/ppermute | solution.py:77
  245.1 1.9 collective-permute-start.1
  247.7 47.8 %collective-permute-done.1 = f32[2,2,64,2160]{3,2,1,0:T(8,128)} collective-permute-done((f32[2,2,64,2160]{3,2,1,0:T(8,128)S(1)}, f32[2,2,64,2160]{3,2,1,0:T(8,128)}, u32[]{:S(2)}, u32[]{:S(2)}) %collective-permute-start.1) | collective-permute-done | bytes 2211872 | tf_op jit(solution)/shard_map/ppermute | solution.py:77
  295.5 2.2 multiply_reduce_fusion.1
  297.8 74.4 %all-reduce = (f32[64]{0:T(128)S(1)}, f32[64]{0:T(128)S(1)}) all-reduce(f32[64]{0:T(128)} %get-tuple-element.4, f32[64]{0:T(128)} %get-tuple-element.3), channel_id=1, replica_groups=mesh['order'=64,'lat'=4] {'order','lat'}, use_global_device_ids=true, to_apply=%region_1.0 | all-reduce | flops 128 | bytes 1024 | tf_op jit(solution)/shard_map/psum | solution.py:36
  372.7 3.3 multiply_reduce_fusion
  376.0 73.3 %psum.23 = f32[64]{0:T(128)S(1)} all-reduce(f32[64]{0:T(128)} %get-tuple-element.7), channel_id=1, replica_groups=mesh['order'=64,'lat'=4] {'order','lat'}, use_global_device_ids=true, to_apply=%region_5.6 | all-reduce | flops 64 | bytes 512 | tf_op jit(solution)/shard_map/psum | solution.py:83
  449.9 1.0 multiply_add_fusion
  (42 shorter events, 4.1 us)
Async XLA Ops:
  7.2 2.5 copy-start
  7.2 2.4 copy-start.10
  7.2 2.5 copy-start.11
  7.2 59.0 %all-gather.2.cloned.1.call-start = ((), (), s32[]{:S(2)}) async-start(), calls=%async_computation.2 | async-start | bytes 5529600 | tf_op jit(solution)/shard_map/all_gather | solution.py:37
  9.7 1.7 copy-start.9
  66.2 6.6 %copy-start.1 = (f32[2,2160,512]{2,1,0:T(8,128)S(1)}, f32[2,2160,512]{2,1,0:T(8,128)}, u32[]{:S(2)}) copy-start(f32[2,2160,512]{2,1,0:T(8,128)} %param.12) | copy-start | bytes 26542084
  72.7 20.7 %copy-start.6 = (f32[8,4320,1]{1,2,0:T(1,128)S(1)}, f32[8,4320,1]{1,2,0:T(1,128)}, u32[]{:S(2)}) copy-start(f32[8,4320,1]{1,2,0:T(1,128)} %get-tuple-element.11) | copy-start | bytes 414724
  72.8 20.7 %copy-start.7 = (s32[8,4320]{1,0:T(8,128)S(1)}, s32[8,4320]{1,0:T(8,128)}, u32[]{:S(2)}) copy-start(s32[8,4320]{1,0:T(8,128)} %param.15) | copy-start | bytes 414724
  82.5 28.5 %all-to-all-start = ((f32[2,512,128]{2,0,1:T(2,128)}), f32[2,512,128]{2,0,1:T(2,128)S(1)}, u32[]{:S(2)}, u32[]{:S(2)}) async-start(f32[2,512,128]{2,0,1:T(2,128)} %copy.22), calls=%async_computation | async-start | bytes 1048576 | tf_op jit(solution)/shard_map/all_to_all | solution.py:43
  113.5 31.3 %copy-start.2 = (f32[1,128,4320]{1,2,0:T(8,128)S(1)}, f32[1,128,4320]{1,2,0:T(8,128)}, u32[]{:S(2)}) copy-start(f32[1,128,4320]{1,2,0:T(8,128)} %get-tuple-element.13) | copy-start | bytes 6635524
  195.0 100.5 %copy-start.3 = (f32[2,2,64,540]{3,2,1,0:T(8,128)S(1)}, f32[2,2,64,540]{3,2,1,0:T(8,128)}, u32[]{:S(2)}) copy-start(f32[2,2,64,540]{3,2,1,0:T(8,128)} %param.11) | copy-start | bytes 1658884
  195.0 100.5 %copy-start.5 = (f32[2,2,64,540]{3,2,1,0:T(8,128)S(1)}, f32[2,2,64,540]{3,2,1,0:T(8,128)}, u32[]{:S(2)}) copy-start(f32[2,2,64,540]{3,2,1,0:T(8,128)} %param.10) | copy-start | bytes 1658884
  195.0 100.5 %copy-start.8 = (f32[540]{0:T(1024)S(1)}, f32[540]{0:T(1024)}, u32[]{:S(2)}) copy-start(f32[540]{0:T(1024)} %param.17) | copy-start | bytes 6484
  195.1 49.7 %collective-permute-start = (f32[2,2,64,2160]{3,2,1,0:T(8,128)S(1)}, f32[2,2,64,2160]{3,2,1,0:T(8,128)S(1)}, u32[]{:S(2)}, u32[]{:S(2)}) collective-permute-start(f32[2,2,64,2160]{3,2,1,0:T(8,128)S(1)} %fusion.2), channel_id=1, source_target_pairs={{0,1},{1,0},{2,3},{3,2},{4,5},{5,4},{6,7},{7,6},{8,9},{9,8},{10,11... | collective-permute-start | bytes 6635528 | tf_op jit(solution)/shard_map/ppermute | solution.py:77
  245.1 50.4 %collective-permute-start.1 = (f32[2,2,64,2160]{3,2,1,0:T(8,128)S(1)}, f32[2,2,64,2160]{3,2,1,0:T(8,128)}, u32[]{:S(2)}, u32[]{:S(2)}) collective-permute-start(f32[2,2,64,2160]{3,2,1,0:T(8,128)S(1)} %add.58), channel_id=1, source_target_pairs={{0,2},{1,3},{2,0},{3,1},{4,6},{5,7},{6,4},{7,5},{8,10},{9,11},{10,... | collective-permute-start | bytes 6635528 | tf_op jit(solution)/shard_map/ppermute | solution.py:77
  372.2 0.5 copy-start.12
  376.0 74.9 %copy-start.4 = (f32[2,2,64,540]{3,2,1,0:T(8,128)}, f32[2,2,64,540]{3,2,1,0:T(8,128)S(1)}, u32[]{:S(2)}) copy-start(f32[2,2,64,540]{3,2,1,0:T(8,128)S(1)} %get-tuple-element.8) | copy-start | bytes 1658884
Sparse Core Ops, SparseCore 0:
  9.8 56.2 all-gather.1
